TPU v7x, 32 devices: a whole 2x2x4 slice. The times are simulated.
32 devices in a mesh: grp: 4 (over y, x), seq: 8 (over z, core).
Axes of the slice: x: 2, y: 2, z: 4, core: 2. Of those that a mesh axis runs over, the one named last changes fastest.
Arguments:
- tokens: bfloat16 [4, 3072, 1536], P('grp', 'seq'), may hold values from -32 to 32, as said below
- router: bfloat16 [1536, 128], P('grp'), may hold values from -1 to 1, as said below
- norm_gain: float32 [8, 1536], P('seq'), may hold values from 0.1 to 1.9
- w_in: bfloat16 [8, 1536, 6144], P('seq', None, 'grp'), may hold values from -0.15625 to 0.15625
- w_out: bfloat16 [8, 6144, 1536], P('seq', 'grp'), may hold values from -0.078125 to 0.078125
Outputs:
- output: bfloat16 [4, 3072, 1536], P('grp', 'seq')
Inputs may be any that keep to these rules, and one draw needn't show every extreme that they name: `tokens`: token features are real values. `router`: slot parameters are real values.
All inputs are finite; a program needn't handle non-finite values.
Results may differ from a plain program's by a relative error of at most 0.0075.
Values may be sent and summed in bfloat16 or wider, within the bound.
A program may use at most 64 MiB of HBM per device.

v0:
```python
import jax
import jax.numpy as jnp
from jax import lax
from jax.sharding import PartitionSpec as P


def local(tokens, router, norm_gain, w_in, w_out):
    feats = tokens[0]
    width = feats.shape[1]
    slot_count = router.shape[1]
    columns = feats
    logits = jnp.dot(
        columns,
        lax.all_gather(router, "grp", axis=0, tiled=True),
        preferred_element_type=jnp.float32,
    )
    owners = lax.axis_size("seq")
    per_owner = slot_count // owners
    local_high = jnp.max(logits, axis=0)
    dispatch = jnp.exp(logits - local_high).astype(jnp.bfloat16)
    partial_sums = lax.dot_general(
        dispatch, feats, (((0,), (0,)), ((), ())), preferred_element_type=jnp.float32
    )
    received, source_highs = (
        lax.all_to_all(
            partial_sums.reshape(owners, per_owner, width),
            "seq",
            split_axis=0,
            concat_axis=0,
            tiled=True,
        ),
        lax.all_to_all(
            local_high.reshape(owners, per_owner), "seq", split_axis=0, concat_axis=0, tiled=True
        ),
    )
    overall = jnp.max(source_highs, axis=0)
    pooled = jnp.sum(received * jnp.exp(source_highs - overall)[:, :, None], axis=0)
    mean_sq = jnp.mean(pooled * pooled, axis=-1, keepdims=True)
    normed = (pooled * lax.rsqrt(mean_sq + 1e-06) * norm_gain[0]).astype(jnp.bfloat16)
    hidden = jax.nn.gelu(
        jnp.dot(
            lax.all_gather(normed, "grp", axis=0, tiled=True),
            w_in[0],
            preferred_element_type=jnp.float32,
        )
    ).astype(jnp.bfloat16)
    partials = jnp.dot(hidden, w_out[0], preferred_element_type=jnp.float32)
    own_out = lax.psum_scatter(
        partials.astype(jnp.bfloat16), "grp", scatter_dimension=0, tiled=True
    )
    weights = jax.nn.softmax(logits, axis=1).astype(jnp.bfloat16)
    columns = weights
    mixed = jnp.dot(
        columns,
        lax.all_gather(own_out, "seq", axis=0, tiled=True),
        preferred_element_type=jnp.float32,
    )
    return (feats.astype(jnp.float32) + mixed).astype(jnp.bfloat16)[None]


def solution(mesh):
    in_specs = (
        P("grp", "seq", None),
        P("grp", None),
        P("seq", None),
        P("seq", None, "grp"),
        P("seq", "grp", None),
    )
    out_specs = P("grp", "seq", None)
    return jax.shard_map(local, mesh=mesh, in_specs=in_specs, out_specs=out_specs, check_vma=False)
```

profile of v0, /device:TPU:0, one launch (start us, length us, event | category | flops | bytes accessed | tf_op | source)
XLA Modules:
  0.0 115.8 jit_solution(2420471679129027630)
XLA Ops:
  6.5 0.0 copy-start
  6.5 11.5 %all_gather.9 = bf16[1536,128]{1,0:T(8,128)(2,1)S(1)} all-gather(bf16[384,128]{1,0:T(8,128)(2,1)} %param.6), channel_id=1, replica_groups=mesh['grp'=4,'seq'=8] {'grp'}, dimensions={0}, use_global_device_ids=true | all-gather | bytes 491520 | tf_op jit(solution)/shard_map/all_gather | solution.py:14
  18.0 1.8 %fusion.38 = (f32[384]{0:T(512)S(1)}, f32[384,128]{0,1:T(8,128)S(1)}) fusion(bf16[1536,128]{1,0:T(8,128)(2,1)S(1)} %all_gather.9, bf16[1,384,1536]{2,1,0:T(8,128)(2,1)} %param.5), kind=kOutput, calls=%fused_computation.40 | convolution fusion | flops 151043712 | bytes 1771008 | tf_op jit(solution)/shard_map/dot_general | solution.py:12
  19.8 0.0 copy-start.1
  19.8 0.1 fusion.31
  19.9 0.7 all_to_all.12
  20.6 4.9 %all-to-all-start.1 = ((f32[8,1,16]{2,1,0:T(1,128)}), f32[8,1,16]{2,1,0:T(1,128)S(1)}, u32[]{:S(2)}, u32[]{:S(2)}) async-start(f32[8,1,16]{2,1,0:T(1,128)} %bitcast.4), calls=%async_computation.1 | async-start | bytes 8192 | tf_op jit(solution)/shard_map/all_to_all | solution.py:32
  25.5 0.1 exponential_convert_fusion
  25.6 0.0 copy-done
  25.6 1.3 %fusion.9 = f32[8,16,1536]{2,1,0:T(8,128)} fusion(bf16[8,16,384]{2,1,0:T(8,128)(2,1)S(1)} %bitcast.34, bf16[1,384,1536]{2,1,0:T(8,128)(2,1)S(1)} %copy-done), kind=kOutput, calls=%fused_computation.8 | convolution fusion | flops 150994944 | bytes 2064384 | tf_op jit(solution)/shard_map/dot_general | solution.py:21
  26.8 4.2 %all-to-all-done.1 = f32[8,1,16]{2,1,0:T(1,128)S(1)} async-done(((f32[8,1,16]{2,1,0:T(1,128)}), f32[8,1,16]{2,1,0:T(1,128)S(1)}, u32[]{:S(2)}, u32[]{:S(2)}) %all-to-all-start.1) | async-done | bytes 544 | tf_op jit(solution)/shard_map/all_to_all | solution.py:32
  31.0 3.5 %all-to-all-start = ((f32[8,16,1536]{2,1,0:T(8,128)}), f32[8,16,1536]{2,1,0:T(8,128)S(1)}, u32[]{:S(2)}, u32[]{:S(2)}) async-start(f32[8,16,1536]{2,1,0:T(8,128)} %fusion.9), calls=%async_computation | async-start | bytes 1572864 | tf_op jit(solution)/shard_map/all_to_all | solution.py:25
  34.6 0.0 reduce-scatter.2.cloned.1.call-start
  34.6 0.0 copy-done.1
  34.7 20.7 %all-to-all-done = f32[8,16,1536]{2,1,0:T(8,128)S(1)} async-done(((f32[8,16,1536]{2,1,0:T(8,128)}), f32[8,16,1536]{2,1,0:T(8,128)S(1)}, u32[]{:S(2)}, u32[]{:S(2)}) %all-to-all-start) | async-done | bytes 786464 | tf_op jit(solution)/shard_map/all_to_all | solution.py:25
  55.5 0.1 multiply_reduce_fusion
  55.6 0.1 multiply_reduce_fusion.1
  55.7 0.1 multiply_convert_fusion
  55.8 8.4 %all_gather.10 = bf16[64,1536]{1,0:T(8,128)(2,1)S(1)} all-gather(bf16[16,1536]{1,0:T(8,128)(2,1)S(1)} %multiply_convert_fusion), channel_id=1, replica_groups=mesh['grp'=4,'seq'=8] {'grp'}, dimensions={0}, use_global_device_ids=true | all-gather | bytes 245760 | tf_op jit(solution)/shard_map/all_gather | solution.py:42
  64.2 6.3 %fusion.6 = bf16[64,1536]{1,0:T(8,128)(2,1)} fusion(bf16[1,1536,1536]{2,1,0:T(8,128)(2,1)} %param.9, bf16[64,1536]{1,0:T(8,128)(2,1)S(1)} %all_gather.10, bf16[1,1536,1536]{2,1,0:T(8,128)(2,1)} %param.8), kind=kOutput, calls=%fused_computation.7 | convolution fusion | flops 604962816 | bytes 9830400 | tf_op jit(solution)/shard_map/dot_general | solution.py:47
  70.4 0.0 reduce-scatter.2.cloned.1.call-update
  70.5 22.3 %reduce-scatter.2.cloned.1.call-done = bf16[16,1536]{1,0:T(8,128)(2,1)} async-done(((bf16[64,1536]{1,0:T(8,128)(2,1)}), bf16[16,1536]{1,0:T(8,128)(2,1)}) %reduce-scatter.2.cloned.1.call-update) | async-done | bytes 49168 | tf_op jit(solution)/shard_map/reduce_scatter | solution.py:48
  92.8 14.7 %all_gather.11 = bf16[128,1536]{1,0:T(8,128)(2,1)S(1)} all-gather(bf16[16,1536]{1,0:T(8,128)(2,1)} %reduce-scatter.2.cloned.1.call-done), channel_id=1, replica_groups=mesh['grp'=4,'seq'=8] {'seq'}, dimensions={0}, use_global_device_ids=true | all-gather | bytes 442368 | tf_op jit(solution)/shard_map/all_gather | solution.py:55
  107.5 1.5 %fusion.5 = bf16[1,384,1536]{2,1,0:T(8,128)(2,1)} fusion(bf16[128,1536]{1,0:T(8,128)(2,1)S(1)} %all_gather.11, bf16[1,384,1536]{2,1,0:T(8,128)(2,1)S(1)} %copy-done, f32[384,128]{0,1:T(8,128)S(1)} %get-tuple-element.8, f32[384]{0:T(512)S(1)} %get-tuple-element.5, f32[384]{0:T(512)S(1)} %get-tuple-element.7), kind=kOutput, calls=%fused_computation.6 | convolution fusion | flops 152911872 | bytes 2952192 | tf_op jit(solution)/shard_map/dot_general | solution.py:53
  (4 shorter events, 0.1 us)
Async XLA Ops:
  6.5 19.0 %copy-start = (bf16[1,384,1536]{2,1,0:T(8,128)(2,1)S(1)}, bf16[1,384,1536]{2,1,0:T(8,128)(2,1)}, u32[]{:S(2)}) copy-start(bf16[1,384,1536]{2,1,0:T(8,128)(2,1)} %param.5) | copy-start | bytes 3538948
  19.8 14.9 %copy-start.1 = (f32[1,1536]{1,0:T(1,128)S(1)}, f32[1,1536]{1,0:T(1,128)}, u32[]{:S(2)}) copy-start(f32[1,1536]{1,0:T(1,128)} %param.7) | copy-start | bytes 18436
  20.6 10.5 %all-to-all-start.1 = ((f32[8,1,16]{2,1,0:T(1,128)}), f32[8,1,16]{2,1,0:T(1,128)S(1)}, u32[]{:S(2)}, u32[]{:S(2)}) async-start(f32[8,1,16]{2,1,0:T(1,128)} %bitcast.4), calls=%async_computation.1 | async-start | bytes 8192 | tf_op jit(solution)/shard_map/all_to_all | solution.py:32
  31.0 24.4 %all-to-all-start = ((f32[8,16,1536]{2,1,0:T(8,128)}), f32[8,16,1536]{2,1,0:T(8,128)S(1)}, u32[]{:S(2)}, u32[]{:S(2)}) async-start(f32[8,16,1536]{2,1,0:T(8,128)} %fusion.9), calls=%async_computation | async-start | bytes 1572864 | tf_op jit(solution)/shard_map/all_to_all | solution.py:25
  34.6 58.2 %reduce-scatter.2.cloned.1.call-start = ((), (), s32[]{:S(2)}) async-start(), calls=%async_computation.3 | async-start | bytes 245760 | tf_op jit(solution)/shard_map/reduce_scatter | solution.py:48
Sparse Core Ops, SparseCore 0:
  70.6 22.1 reduce-scatter.1
where the time goes:
time: 116 us
  waiting for transfers between devices  47.3 us (41%)
  blocking collectives  34.5 us (30%)
  between operations  13.5 us (12%)
  matrix products  10.8 us (9%)
  starting transfers between devices  8.47 us (7%)
    reduce_scatter x1, waiting for transfers between devices, local(): lax.psum_scatter(partials.astype(jnp.bfloat16), 'grp', scatter_dimension=...  22.3 us
    all_to_all x1, waiting for transfers between devices, local(): lax.all_to_all(partial_sums.reshape(owners, per_owner, width), 'seq', spl...  20.7 us
    all_gather x1, blocking collectives, local(): lax.all_gather(own_out, 'seq', axis=0, tiled=True)  14.7 us
    all_gather x1, blocking collectives, local(): lax.all_gather(router, 'grp', axis=0, tiled=True)  11.5 us
    all_gather x1, blocking collectives, local(): lax.all_gather(normed, 'grp', axis=0, tiled=True)  8.36 us
    dot_general x1, matrix products, local(): partials = jnp.dot(hidden, w_out[0], preferred_element_type=jnp.float32)  6.26 us
    all_to_all x1, starting transfers between devices, local(): lax.all_to_all(local_high.reshape(owners, per_owner), 'seq', split_axis=0...  4.88 us
    all_to_all x1, waiting for transfers between devices, local(): lax.all_to_all(local_high.reshape(owners, per_owner), 'seq', split_axis=0...  4.2 us
  transfers between devices with their start and end apart: 3, of which 3 were waited for; matrix products, arithmetic and copies ran while one was open for 1% of the time, Pallas kernels for 0%

commit v1 on v0

v1 whole, which is shorter than its diff:
```python
import functools

import jax
import jax.numpy as jnp
from jax import lax
from jax.experimental import pallas as pl
from jax.experimental.pallas import tpu as pltpu
from jax.sharding import PartitionSpec as P

F32, BF16 = jnp.float32, jnp.bfloat16
LANES = 128


def tile_of(n):
    for t in (512, 384, 256, 128):
        if n % t == 0:
            return t
    return n


def remote(src, dst, send, recv, g, e):
    return pltpu.make_async_remote_copy(
        src_ref=src, dst_ref=dst, send_sem=send, recv_sem=recv,
        device_id={"grp": g, "seq": e}, device_id_type=pl.DeviceIdType.MESH,
    )


def kernel(G, S, tok_h, rt_h, gain, wi_h, wo_h, eo, wts,
           tok, rt, wi, wo, logits, dT, pf, pb, xb, hp, hpc, hz, hzc, cown, sb, zb,
           pool, gath, hid, part, rs, eown,
           loc, a_s, a_r, f_s, f_r, p_s, p_r, h_s, h_r, z_s, z_r, zh_s, zh_r,
           n_s, n_r, r_s, r_r, e_s, e_r, ef_s, ef_r):
    g, e = lax.axis_index("grp"), lax.axis_index("seq")
    Z = S // 2
    z, k = e // 2, e % 2
    partner = e + 1 - 2 * k
    rows = rt_h.shape[0]
    half = rows // 2
    T, D = tok.shape
    SL = rt.shape[1]
    E = SL // S
    FF = wi.shape[1]
    tn = tile_of(D)
    NT = D // tn
    tf = tile_of(FF)
    cols = [pl.ds(t * tn, tn) for t in range(NT)]

    def rsl(gg, kk):
        return pl.ds(pl.multiple_of(gg * rows + kk * half, 16), half)

    c_rt = pltpu.make_async_copy(rt_h, rt.at[pl.ds(pl.multiple_of(g * rows, 16), rows)], loc.at[0])
    c_tok = pltpu.make_async_copy(tok_h.at[0], tok, loc.at[1])
    c_wi = pltpu.make_async_copy(wi_h.at[0], wi, loc.at[2])
    c_wo = pltpu.make_async_copy(wo_h.at[0], wo, loc.at[3])
    c_rt.start()
    c_tok.start()
    hp[...] = jnp.zeros_like(hp)
    hz[...] = jnp.zeros_like(hz)

    bar = pltpu.get_barrier_semaphore()

    def greet(gg, ee):
        pl.semaphore_signal(bar, inc=1, device_id={"grp": gg, "seq": ee},
                            device_id_type=pl.DeviceIdType.MESH)

    def gpeer(d):
        return lax.rem(g + d, G)

    def gfrom(d):
        return lax.rem(g - d + G, G)

    def zpeer(d):
        return lax.rem(z + d, Z)

    def zfrom(d):
        return lax.rem(z - d + Z, Z)

    greet(g, partner)
    for d in range(1, G):
        greet(gpeer(d), e)
    for d in range(1, Z):
        greet(g, zpeer(d) * 2 + k)
    pl.semaphore_wait(bar, G + Z - 1)

    pend = []

    ksl = pl.ds(pl.multiple_of(k * half, 16), half)
    for d in range(1, G):
        c = remote(rt_h.at[ksl], rt.at[rsl(g, k)], a_s.at[d], a_r.at[d], gpeer(d), e)
        c.start()
        pend.append(c)
    c_wi.start()
    c_wo.start()
    for d in range(1, G):
        sl = rt.at[rsl(gfrom(d), k)]
        remote(sl, sl, a_s.at[d], a_r.at[d], g, partner).wait_recv()
        c = remote(sl, sl, f_s.at[d], f_r.at[d], g, partner)
        c.start()
        pend.append(c)
    for d in range(1, G):
        sl = rt.at[rsl(gfrom(d), 1 - k)]
        remote(sl, sl, f_s.at[d], f_r.at[d], g, partner).wait_recv()
    c_rt.wait()
    c_tok.wait()

    lg = jnp.dot(tok[...], rt[...], preferred_element_type=F32)
    high = jnp.max(lg, axis=0, keepdims=True)
    hp[0:1] = high
    c_h = remote(hp.at[pl.ds(0, 1)], hp.at[pl.ds(1, 1)], h_s, h_r, g, partner)
    c_h.start()
    pend.append(c_h)
    logits[...] = lg
    dT[...] = jnp.transpose(jnp.exp(lg - high)).astype(BF16)

    pair = []
    for t in range(NT):
        ps = jnp.dot(dT[...], tok[:, cols[t]], preferred_element_type=F32).reshape(Z, 2, E, tn)
        pf[:, :, :, cols[t]] = ps
        pb[:, :, :, cols[t]] = ps.astype(BF16)
        c = remote(pb.at[:, 1 - k, :, cols[t]], xb.at[:, :, cols[t]], p_s.at[t], p_r.at[t], g, partner)
        c.start()
        pair.append(c)

    c_h.wait_recv()
    hh = hp[...]
    hm = jnp.maximum(hh[0:1], hh[1:2])
    hpc[...] = jnp.transpose(jnp.exp(jnp.minimum(hh - hm, 0.0))).reshape(Z, 2, E, LANES)
    hz[0:1] = hm
    for d in range(1, Z):
        c = remote(hz.at[pl.ds(0, 1)], hz.at[pl.ds(d, 1)], zh_s.at[d], zh_r.at[d], g, zpeer(d) * 2 + k)
        c.start()
        pend.append(c)
    for t in range(NT):
        pair[t].wait_recv()
        for d in range(Z - 1, -1, -1):
            zz = zpeer(d)
            fac = hpc[zz, k]
            v = pf[zz, k, :, cols[t]] * fac[:, 0:1] + xb[zz, :, cols[t]].astype(F32) * fac[:, 1:2]
            if d == 0:
                cown[:, cols[t]] = v
            else:
                sb[d, :, cols[t]] = v.astype(BF16)
                c = remote(sb.at[d, :, cols[t]], zb.at[d, :, cols[t]], z_s.at[d, t], z_r.at[d, t],
                           g, zz * 2 + k)
                c.start()
                pend.append(c)
    for c in pair:
        c.wait_send()

    lg = logits[...]
    ex = jnp.exp(lg - jnp.max(lg, axis=1, keepdims=True))
    wts[...] = (ex / jnp.sum(ex, axis=1, keepdims=True)).astype(BF16)

    for d in range(1, Z):
        sl = hz.at[pl.ds(d, 1)]
        remote(sl, sl, zh_s.at[d], zh_r.at[d], g, e).wait_recv()
    hh = hz[...]
    top = jnp.max(hh[0:Z], axis=0, keepdims=True)
    hzc[...] = jnp.transpose(jnp.exp(jnp.minimum(hh - top, 0.0))).reshape(S, E, LANES)
    fac = hzc[e]
    sq = jnp.zeros((E, 1), F32)
    for t in range(NT):
        v = cown[:, cols[t]] * fac[:, 0:1]
        for d in range(1, Z):
            sl = zb.at[d, :, cols[t]]
            remote(sl, sl, z_s.at[d, t], z_r.at[d, t], g, e).wait_recv()
            v = v + zb[d, :, cols[t]].astype(F32) * fac[:, d:d + 1]
        pool[:, cols[t]] = v
        sq = sq + jnp.sum(v * v, axis=1, keepdims=True)
    inv = lax.rsqrt(sq / D + 1e-06)
    gath[g] = (pool[...] * inv * gain[...]).astype(BF16)
    for d in range(1, G):
        c = remote(gath.at[g], gath.at[g], n_s.at[d], n_r.at[d], gpeer(d), e)
        c.start()
        pend.append(c)
    c_wi.wait()
    c_wo.wait()
    for d in range(1, G):
        sl = gath.at[gfrom(d)]
        remote(sl, sl, n_s.at[d], n_r.at[d], g, e).wait_recv()

    x = gath[...].reshape(G * E, D)
    for t in range(FF // tf):
        fs = pl.ds(t * tf, tf)
        hid[:, fs] = jax.nn.gelu(jnp.dot(x, wi[:, fs], preferred_element_type=F32)).astype(BF16)
    hd = hid[...]
    for t in range(NT):
        part[:, :, cols[t]] = jnp.dot(hd, wo[:, cols[t]], preferred_element_type=F32).astype(BF16).reshape(G, E, tn)
        for d in range(1, G):
            c = remote(part.at[gpeer(d), :, cols[t]], rs.at[d, :, cols[t]], r_s.at[d, t], r_r.at[d, t],
                       gpeer(d), e)
            c.start()
            pend.append(c)

    own = []
    for t in range(NT):
        v = part[g, :, cols[t]].astype(F32)
        for d in range(1, G):
            sl = rs.at[d, :, cols[t]]
            remote(sl, sl, r_s.at[d, t], r_r.at[d, t], g, e).wait_recv()
            v = v + rs[d, :, cols[t]].astype(F32)
        eown[:, cols[t]] = v.astype(BF16)
        src, dst = eown.at[:, cols[t]], eo.at[e, :, cols[t]]
        for d in range(Z - 1, 0, -1):
            c = remote(src, dst, e_s.at[d, t], e_r.at[d, t], g, zpeer(d) * 2 + k)
            c.start()
            pend.append(c)
        c = remote(src, dst, ef_s.at[0, t], ef_r.at[0, t], g, partner)
        c.start()
        pend.append(c)
        c = pltpu.make_async_copy(src, dst, e_s.at[0, t])
        c.start()
        own.append(c)
    for t in range(NT):
        for d in range(1, Z):
            sl = eo.at[zfrom(d) * 2 + k, :, cols[t]]
            remote(sl, sl, e_s.at[d, t], e_r.at[d, t], g, e).wait_recv()
            c = remote(sl, sl, ef_s.at[d, t], ef_r.at[d, t], g, partner)
            c.start()
            pend.append(c)
    for t in range(NT):
        own[t].wait()
        for d in range(Z):
            sl = eo.at[zfrom(d) * 2 + 1 - k, :, cols[t]]
            remote(sl, sl, ef_s.at[d, t], ef_r.at[d, t], g, e).wait_recv()
    for c in pend:
        c.wait_send()


def local(G, S, tokens, router, norm_gain, w_in, w_out):
    _, T, D = tokens.shape
    rows, SL = router.shape
    E, Z = SL // S, S // 2
    FF = w_in.shape[2]
    NT = D // tile_of(D)
    anyspace = pl.BlockSpec(memory_space=pl.ANY)
    vmem = pl.BlockSpec(memory_space=pltpu.VMEM)
    dma = lambda *s: pltpu.SemaphoreType.DMA(s)
    eo, wts = pl.pallas_call(
        functools.partial(kernel, G, S),
        out_shape=(jax.ShapeDtypeStruct((S, E, D), BF16), jax.ShapeDtypeStruct((T, SL), BF16)),
        in_specs=[anyspace, anyspace, vmem, anyspace, anyspace],
        out_specs=(anyspace, vmem),
        scratch_shapes=[
            pltpu.VMEM((T, D), BF16),
            pltpu.VMEM((rows * G, SL), BF16),
            pltpu.VMEM((D, FF), BF16),
            pltpu.VMEM((FF, D), BF16),
            pltpu.VMEM((T, SL), F32),
            pltpu.VMEM((SL, T), BF16),
            pltpu.VMEM((Z, 2, E, D), F32),
            pltpu.VMEM((Z, 2, E, D), BF16),
            pltpu.VMEM((Z, E, D), BF16),
            pltpu.VMEM((LANES, SL), F32),
            pltpu.VMEM((Z, 2, E, LANES), F32),
            pltpu.VMEM((LANES, SL), F32),
            pltpu.VMEM((S, E, LANES), F32),
            pltpu.VMEM((E, D), F32),
            pltpu.VMEM((Z, E, D), BF16),
            pltpu.VMEM((Z, E, D), BF16),
            pltpu.VMEM((E, D), F32),
            pltpu.VMEM((G, E, D), BF16),
            pltpu.VMEM((G * E, FF), BF16),
            pltpu.VMEM((G, E, D), BF16),
            pltpu.VMEM((G, E, D), BF16),
            pltpu.VMEM((E, D), BF16),
            dma(4), dma(G), dma(G), dma(G), dma(G), dma(NT), dma(NT),
            pltpu.SemaphoreType.DMA, pltpu.SemaphoreType.DMA,
            dma(Z, NT), dma(Z, NT), dma(Z), dma(Z),
            dma(G), dma(G), dma(G, NT), dma(G, NT),
            dma(Z, NT), dma(Z, NT), dma(Z, NT), dma(Z, NT),
        ],
        compiler_params=pltpu.CompilerParams(
            collective_id=0, has_side_effects=True, vmem_limit_bytes=48 * 1024 * 1024
        ),
    )(tokens, router, norm_gain, w_in, w_out)
    mixed = jnp.dot(wts, eo.reshape(SL, D), preferred_element_type=F32)
    return (tokens[0].astype(F32) + mixed).astype(BF16)[None]


def solution(mesh):
    in_specs = (
        P("grp", "seq", None),
        P("grp", None),
        P("seq", None),
        P("seq", None, "grp"),
        P("seq", "grp", None),
    )
    out_specs = P("grp", "seq", None)
    f = functools.partial(local, mesh.shape["grp"], mesh.shape["seq"])
    return jax.shard_map(f, mesh=mesh, in_specs=in_specs, out_specs=out_specs, check_vma=False)
```

time: 116 us -> 39.5 us (0.34)
  waiting for transfers between devices: 47.3 us -> 0 us
  Pallas kernels: 0 us -> 34.9 us
  blocking collectives: 34.5 us -> 0 us
  between operations: 13.5 us -> 0.01 us
  matrix products: 10.8 us -> 1.47 us
  starting transfers between devices: 8.47 us -> 0 us
  local copies, waits for them, and re-layouts: 0.69 us -> 2.85 us
    pallas_call x0 -> x1, Pallas kernels: none -> 34.9 us  [local(): pl.pallas_call(functools.partial(kernel, G, S), out_shape=(jax.ShapeDtype...]
    all_gather x3 -> x0, blocking collectives: 34.5 us -> none  [the longest x1 14.7 us: local(): lax.all_gather(own_out, 'seq', axis=0, tiled=True)]
    all_to_all x2 -> x0, waiting for transfers between devices: 24.9 us -> none  [the longest x1 20.7 us: local(): lax.all_to_all(partial_sums.reshape(owners, per_owner, width), 'seq', spl...]
    reduce_scatter x1 -> x0, waiting for transfers between devices: 22.3 us -> none  [local(): lax.psum_scatter(partials.astype(jnp.bfloat16), 'grp', scatter_dimension=...]
    dot_general x4 -> x1, matrix products: 10.8 us -> 1.47 us  [local(): mixed = jnp.dot(wts, eo.reshape(SL, D), preferred_element_type=F32)]
    all_to_all x2 -> x0, starting transfers between devices: 8.43 us -> none  [the longest x1 4.88 us: local(): lax.all_to_all(local_high.reshape(owners, per_owner), 'seq', split_axis=0...]
    unnamed x4 -> x6, local copies, waits for them, and re-layouts: 0.01 us -> 2.85 us
  transfers between devices with their start and end apart: 3 -> 0, of which waited for: 3 -> 0; matrix products, arithmetic and copies ran while one was open for 1% -> 0% of each run, Pallas kernels for 0% -> 0%
where the time goes in v1:
time: 39.5 us; the launch traced here: 39.3 us
  Pallas kernels  34.9 us (88%)
  local copies, waits for them, and re-layouts  2.85 us (7%)
  matrix products  1.47 us (4%)
    pallas_call x1, Pallas kernels, local(): pl.pallas_call(functools.partial(kernel, G, S), out_shape=(jax.ShapeDtype...  34.9 us
    unnamed x6, local copies, waits for them, and re-layouts  2.85 us
    dot_general x1, matrix products, local(): mixed = jnp.dot(wts, eo.reshape(SL, D), preferred_element_type=F32)  1.47 us

profile of v1, /device:TPU:0, one launch (start us, length us, event | category | flops | bytes accessed | tf_op | source)
XLA Modules:
  0.0 39.3 jit_solution(14124180154233711337)
XLA Ops:
  0.0 0.0 copy-start
  0.0 1.3 %copy-done = bf16[1,384,1536]{2,1,0:T(8,128)(2,1)S(1)} copy-done((bf16[1,384,1536]{2,1,0:T(8,128)(2,1)S(1)}, bf16[1,384,1536]{2,1,0:T(8,128)(2,1)}, u32[]{:S(2)}) %copy-start) | copy-done | bytes 1179672
  1.3 0.0 copy-start.1
  1.3 0.9 %copy-done.1 = bf16[384,128]{1,0:T(8,128)(2,1)S(1)} copy-done((bf16[384,128]{1,0:T(8,128)(2,1)S(1)}, bf16[384,128]{1,0:T(8,128)(2,1)}, u32[]{:S(2)}) %copy-start.1) | copy-done | bytes 98328
  2.2 0.0 copy-start.2
  2.2 0.7 %copy-done.2 = f32[1,1536]{1,0:T(1,128)S(1)} copy-done((f32[1,1536]{1,0:T(1,128)S(1)}, f32[1,1536]{1,0:T(1,128)}, u32[]{:S(2)}) %copy-start.2) | copy-done | bytes 6168
  2.9 34.9 %shard_map.55 = (bf16[8,16,1536]{2,1,0:T(8,128)(2,1)S(1)}, bf16[384,128]{1,0:T(8,128)(2,1)S(1)}) custom-call(bf16[1,384,1536]{2,1,0:T(8,128)(2,1)S(1)} %copy-done, bf16[384,128]{1,0:T(8,128)(2,1)S(1)} %copy-done.1, f32[1,1536]{1,0:T(1,128)S(1)} %copy-done.2, bf16[1,1536,1536]{2,1,0:T(8,128)(2,1)} %wi_h.1, bf16[1,1536,1536]{2,1,0:T(8,128)(2,1)} %wo_h.1), custom_call_target="tpu_custom_call" | custom-call | tf_op jit(solution)/shard_map/pallas_call | solution.py:239
  37.8 1.5 %fusion.1 = bf16[1,384,1536]{2,1,0:T(8,128)(2,1)} fusion(bf16[384,128]{1,0:T(8,128)(2,1)S(1)} %get-tuple-element.7, bf16[128,1536]{1,0:T(8,128)(2,1)S(1)} %bitcast.8, bf16[1,384,1536]{2,1,0:T(8,128)(2,1)S(1)} %copy-done), kind=kOutput, calls=%fused_computation.2 | convolution fusion | flops 152764416 | bytes 2850816 | tf_op jit(solution)/shard_map/dot_general | solution.py:277
Async XLA Ops:
  0.0 1.3 %copy-start = (bf16[1,384,1536]{2,1,0:T(8,128)(2,1)S(1)}, bf16[1,384,1536]{2,1,0:T(8,128)(2,1)}, u32[]{:S(2)}) copy-start(bf16[1,384,1536]{2,1,0:T(8,128)(2,1)} %tok_h.1) | copy-start | bytes 3538948
  1.3 0.9 %copy-start.1 = (bf16[384,128]{1,0:T(8,128)(2,1)S(1)}, bf16[384,128]{1,0:T(8,128)(2,1)}, u32[]{:S(2)}) copy-start(bf16[384,128]{1,0:T(8,128)(2,1)} %rt_h.1) | copy-start | bytes 294916
  2.2 0.7 %copy-start.2 = (f32[1,1536]{1,0:T(1,128)S(1)}, f32[1,1536]{1,0:T(1,128)}, u32[]{:S(2)}) copy-start(f32[1,1536]{1,0:T(1,128)} %gain.1) | copy-start | bytes 18436

commit v2 on v1

--- a/solution.py
+++ b/solution.py
@@ -9,6 +9,7 @@
 
 F32, BF16 = jnp.float32, jnp.bfloat16
 LANES = 128
+VLIM = 60 * 1024 * 1024
 
 
 def tile_of(n):
@@ -18,6 +19,15 @@
     return n
 
 
+def flip(i, d):
+    out, b = i, 1
+    while b <= d:
+        if d & b:
+            out = out + b * (1 - 2 * ((i // b) % 2))
+        b *= 2
+    return out
+
+
 def remote(src, dst, send, recv, g, e):
     return pltpu.make_async_remote_copy(
         src_ref=src, dst_ref=dst, send_sem=send, recv_sem=recv,
@@ -25,11 +35,11 @@
     )
 
 
-def kernel(G, S, tok_h, rt_h, gain, wi_h, wo_h, eo, wts,
-           tok, rt, wi, wo, logits, dT, pf, pb, xb, hp, hpc, hz, hzc, cown, sb, zb,
-           pool, gath, hid, part, rs, eown,
+def kernel(G, S, tok_h, rt_h, gain_h, wi_h, wo_h, eo, wts,
+           tok, rt, gain, wi, wo, logits, dT, pf, pb, xb, hp, hpc, hz, hzc, cown, sb, zb,
+           ninv, acc, gath, hid, part, rs, eown,
            loc, a_s, a_r, f_s, f_r, p_s, p_r, h_s, h_r, z_s, z_r, zh_s, zh_r,
-           n_s, n_r, r_s, r_r, e_s, e_r, ef_s, ef_r):
+           n_s, n_r, i_s, i_r, r_s, r_r, e_s, e_r, ef_s, ef_r):
     g, e = lax.axis_index("grp"), lax.axis_index("seq")
     Z = S // 2
     z, k = e // 2, e % 2
@@ -54,6 +64,8 @@
     c_wo = pltpu.make_async_copy(wo_h.at[0], wo, loc.at[3])
     c_rt.start()
     c_tok.start()
+    c_gain = pltpu.make_async_copy(gain_h, gain, loc.at[4])
+    c_gain.start()
     hp[...] = jnp.zeros_like(hp)
     hz[...] = jnp.zeros_like(hz)
 
@@ -64,16 +76,20 @@
                             device_id_type=pl.DeviceIdType.MESH)
 
     def gpeer(d):
-        return lax.rem(g + d, G)
+        return flip(g, d)
 
     def gfrom(d):
-        return lax.rem(g - d + G, G)
+        return flip(g, d)
+
+    def chunk(gg):
+        at = pl.ds(pl.multiple_of(gg * rows, LANES), rows)
+        return jnp.dot(tok[:, at], rt[at, :], preferred_element_type=F32)
 
     def zpeer(d):
-        return lax.rem(z + d, Z)
+        return flip(z, d)
 
     def zfrom(d):
-        return lax.rem(z - d + Z, Z)
+        return flip(z, d)
 
     greet(g, partner)
     for d in range(1, G):
@@ -85,7 +101,7 @@
     pend = []
 
     ksl = pl.ds(pl.multiple_of(k * half, 16), half)
-    for d in range(1, G):
+    for d in range(G - 1, 0, -1):
         c = remote(rt_h.at[ksl], rt.at[rsl(g, k)], a_s.at[d], a_r.at[d], gpeer(d), e)
         c.start()
         pend.append(c)
@@ -97,13 +113,19 @@
         c = remote(sl, sl, f_s.at[d], f_r.at[d], g, partner)
         c.start()
         pend.append(c)
+    if not rows % LANES:
+        c_rt.wait()
+        c_tok.wait()
+        lg = chunk(g)
     for d in range(1, G):
         sl = rt.at[rsl(gfrom(d), 1 - k)]
         remote(sl, sl, f_s.at[d], f_r.at[d], g, partner).wait_recv()
-    c_rt.wait()
-    c_tok.wait()
-
-    lg = jnp.dot(tok[...], rt[...], preferred_element_type=F32)
+        if not rows % LANES:
+            lg = lg + chunk(gfrom(d))
+    if rows % LANES:
+        c_rt.wait()
+        c_tok.wait()
+        lg = jnp.dot(tok[...], rt[...], preferred_element_type=F32)
     high = jnp.max(lg, axis=0, keepdims=True)
     hp[0:1] = high
     c_h = remote(hp.at[pl.ds(0, 1)], hp.at[pl.ds(1, 1)], h_s, h_r, g, partner)
@@ -159,34 +181,50 @@
     hzc[...] = jnp.transpose(jnp.exp(jnp.minimum(hh - top, 0.0))).reshape(S, E, LANES)
     fac = hzc[e]
     sq = jnp.zeros((E, 1), F32)
+    c_gain.wait()
     for t in range(NT):
         v = cown[:, cols[t]] * fac[:, 0:1]
         for d in range(1, Z):
             sl = zb.at[d, :, cols[t]]
             remote(sl, sl, z_s.at[d, t], z_r.at[d, t], g, e).wait_recv()
             v = v + zb[d, :, cols[t]].astype(F32) * fac[:, d:d + 1]
-        pool[:, cols[t]] = v
+        gath[g, :, cols[t]] = (v * gain[:, cols[t]]).astype(BF16)
+        sl = gath.at[g, :, cols[t]]
+        for d in range(G - 1, 0, -1):
+            c = remote(sl, sl, n_s.at[d, t], n_r.at[d, t], gpeer(d), e)
+            c.start()
+            pend.append(c)
         sq = sq + jnp.sum(v * v, axis=1, keepdims=True)
-    inv = lax.rsqrt(sq / D + 1e-06)
-    gath[g] = (pool[...] * inv * gain[...]).astype(BF16)
+    ninv[g] = jnp.broadcast_to(lax.rsqrt(sq / D + 1e-06), (E, LANES))
     for d in range(1, G):
-        c = remote(gath.at[g], gath.at[g], n_s.at[d], n_r.at[d], gpeer(d), e)
+        c = remote(ninv.at[g], ninv.at[g], i_s.at[d], i_r.at[d], gpeer(d), e)
         c.start()
         pend.append(c)
     c_wi.wait()
     c_wo.wait()
-    for d in range(1, G):
-        sl = gath.at[gfrom(d)]
-        remote(sl, sl, n_s.at[d], n_r.at[d], g, e).wait_recv()
-
-    x = gath[...].reshape(G * E, D)
-    for t in range(FF // tf):
-        fs = pl.ds(t * tf, tf)
-        hid[:, fs] = jax.nn.gelu(jnp.dot(x, wi[:, fs], preferred_element_type=F32)).astype(BF16)
+    for t in range(NT):
+        for d in range(1, G):
+            sl = gath.at[gfrom(d), :, cols[t]]
+            remote(sl, sl, n_s.at[d, t], n_r.at[d, t], g, e).wait_recv()
+        x = gath[:, :, cols[t]].reshape(G * E, tn)
+        if t == NT - 1:
+            for d in range(1, G):
+                sl = ninv.at[gfrom(d)]
+                remote(sl, sl, i_s.at[d], i_r.at[d], g, e).wait_recv()
+            inv = ninv[...].reshape(G * E, LANES)[:, 0:1]
+        for f in range(FF // tf):
+            fs = pl.ds(f * tf, tf)
+            y = jnp.dot(x, wi[cols[t], fs], preferred_element_type=F32)
+            if t:
+                y = y + acc[:, fs]
+            if t == NT - 1:
+                hid[:, fs] = jax.nn.gelu(y * inv).astype(BF16)
+            else:
+                acc[:, fs] = y
     hd = hid[...]
     for t in range(NT):
         part[:, :, cols[t]] = jnp.dot(hd, wo[:, cols[t]], preferred_element_type=F32).astype(BF16).reshape(G, E, tn)
-        for d in range(1, G):
+        for d in range(G - 1, 0, -1):
             c = remote(part.at[gpeer(d), :, cols[t]], rs.at[d, :, cols[t]], r_s.at[d, t], r_r.at[d, t],
                        gpeer(d), e)
             c.start()
@@ -234,16 +272,18 @@
     FF = w_in.shape[2]
     NT = D // tile_of(D)
     anyspace = pl.BlockSpec(memory_space=pl.ANY)
+    hbm = pl.BlockSpec(memory_space=pltpu.HBM)
     vmem = pl.BlockSpec(memory_space=pltpu.VMEM)
     dma = lambda *s: pltpu.SemaphoreType.DMA(s)
     eo, wts = pl.pallas_call(
         functools.partial(kernel, G, S),
         out_shape=(jax.ShapeDtypeStruct((S, E, D), BF16), jax.ShapeDtypeStruct((T, SL), BF16)),
-        in_specs=[anyspace, anyspace, vmem, anyspace, anyspace],
+        in_specs=[hbm] * 5,
         out_specs=(anyspace, vmem),
         scratch_shapes=[
             pltpu.VMEM((T, D), BF16),
             pltpu.VMEM((rows * G, SL), BF16),
+            pltpu.VMEM((1, D), F32),
             pltpu.VMEM((D, FF), BF16),
             pltpu.VMEM((FF, D), BF16),
             pltpu.VMEM((T, SL), F32),
@@ -258,20 +298,21 @@
             pltpu.VMEM((E, D), F32),
             pltpu.VMEM((Z, E, D), BF16),
             pltpu.VMEM((Z, E, D), BF16),
-            pltpu.VMEM((E, D), F32),
+            pltpu.VMEM((G, E, LANES), F32),
+            pltpu.VMEM((G * E, FF), F32),
             pltpu.VMEM((G, E, D), BF16),
             pltpu.VMEM((G * E, FF), BF16),
             pltpu.VMEM((G, E, D), BF16),
             pltpu.VMEM((G, E, D), BF16),
             pltpu.VMEM((E, D), BF16),
-            dma(4), dma(G), dma(G), dma(G), dma(G), dma(NT), dma(NT),
+            dma(5), dma(G), dma(G), dma(G), dma(G), dma(NT), dma(NT),
             pltpu.SemaphoreType.DMA, pltpu.SemaphoreType.DMA,
             dma(Z, NT), dma(Z, NT), dma(Z), dma(Z),
-            dma(G), dma(G), dma(G, NT), dma(G, NT),
+            dma(G, NT), dma(G, NT), dma(G), dma(G), dma(G, NT), dma(G, NT),
             dma(Z, NT), dma(Z, NT), dma(Z, NT), dma(Z, NT),
         ],
         compiler_params=pltpu.CompilerParams(
-            collective_id=0, has_side_effects=True, vmem_limit_bytes=48 * 1024 * 1024
+            collective_id=0, has_side_effects=True, vmem_limit_bytes=VLIM
         ),
     )(tokens, router, norm_gain, w_in, w_out)
     mixed = jnp.dot(wts, eo.reshape(SL, D), preferred_element_type=F32)

time: 39.5 us -> 37 us (0.937)
  local copies, waits for them, and re-layouts: 2.85 us -> 0.01 us
  matrix products: 1.47 us -> 2.52 us
  Pallas kernels: 34.9 us -> 34.3 us
    unnamed x6 -> x2, local copies, waits for them, and re-layouts: 2.85 us -> 0.01 us
    dot_general x1, matrix products: 1.47 us -> 2.52 us  [local(): mixed = jnp.dot(wts, eo.reshape(SL, D), preferred_element_type=F32)]
    pallas_call x1, Pallas kernels: 34.9 us -> 34.3 us  [local(): pl.pallas_call(functools.partial(kernel, G, S), out_shape=(jax.ShapeDtype...]
where the time goes in v2:
time: 37 us; the launch traced here: 36.8 us
  Pallas kernels  34.3 us (93%)
  matrix products  2.52 us (7%)
    pallas_call x1, Pallas kernels, local(): pl.pallas_call(functools.partial(kernel, G, S), out_shape=(jax.ShapeDtype...  34.3 us
    dot_general x1, matrix products, local(): mixed = jnp.dot(wts, eo.reshape(SL, D), preferred_element_type=F32)  2.52 us

profile of v2, /device:TPU:0, one launch (start us, length us, event | category | flops | bytes accessed | tf_op | source)
XLA Modules:
  0.0 36.8 jit_solution(12353032482095583366)
XLA Ops:
  0.0 0.0 copy-start
  0.0 34.3 %shard_map.55 = (bf16[8,16,1536]{2,1,0:T(8,128)(2,1)}, bf16[384,128]{1,0:T(8,128)(2,1)}) custom-call(bf16[1,384,1536]{2,1,0:T(8,128)(2,1)} %tok_h.1, bf16[384,128]{1,0:T(8,128)(2,1)} %rt_h.1, f32[1,1536]{1,0:T(1,128)} %gain_h.1, bf16[1,1536,1536]{2,1,0:T(8,128)(2,1)} %wi_h.1, bf16[1,1536,1536]{2,1,0:T(8,128)(2,1)} %wo_h.1), custom_call_target="tpu_custom_call" | custom-call | tf_op jit(solution)/shard_map/pallas_call | solution.py:278
  34.3 0.0 copy-done
  34.3 2.5 %fusion.1 = bf16[1,384,1536]{2,1,0:T(8,128)(2,1)} fusion(bf16[384,128]{1,0:T(8,128)(2,1)} %get-tuple-element.7, bf16[128,1536]{1,0:T(8,128)(2,1)} %bitcast.8, bf16[1,384,1536]{2,1,0:T(8,128)(2,1)S(1)} %copy-done), kind=kOutput, calls=%fused_computation.2 | convolution fusion | flops 152764416 | bytes 2850816 | tf_op jit(solution)/shard_map/dot_general | solution.py:318
Async XLA Ops:
  0.0 34.3 %copy-start = (bf16[1,384,1536]{2,1,0:T(8,128)(2,1)S(1)}, bf16[1,384,1536]{2,1,0:T(8,128)(2,1)}, u32[]{:S(2)}) copy-start(bf16[1,384,1536]{2,1,0:T(8,128)(2,1)} %tok_h.1) | copy-start | bytes 3538948
